TPU v7x, 256 devices: a whole 4x4x8 slice. The times are simulated.
256 devices in a mesh: dp: 32 (over y, z), cent: 8 (over x, core).
Axes of the slice: x: 4, y: 4, z: 8, core: 2. Of those that a mesh axis runs over, the one named last changes fastest.
Arguments:
- embeddings: bfloat16 [16384, 768], P('dp'), may hold values from -400 to 400, as said below
- centroids: bfloat16 [16384, 768], P('cent'), may hold values from -400 to 400, as said below
Outputs:
- new_centroids: float32 [16384, 768], P(('cent', 'dp'))
Inputs may be any that keep to these rules, and one draw needn't show every extreme that they name: `embeddings`: finite real values. `centroids`: finite real values.
All inputs are finite; a program needn't handle non-finite values.
Results may differ from a plain program's by a relative error of at most 0.0038.
Values sent between devices are 32-bit elements; how exact they have to be, the bound alone decides.
A program may use at most 64 MiB of HBM per device.

v0:
```python
import jax
import jax.numpy as jnp
from jax import lax
from jax.sharding import PartitionSpec as P

FEATURE_DIM = 768
ROUNDS = 2
entropy_regularizer = 0.05


def normalize(values):
    wide = values.astype(jnp.float32)
    meansq = jnp.mean(wide * wide, axis=-1, keepdims=True)
    return (wide * lax.rsqrt(meansq + 1e-06)).astype(jnp.bfloat16)


def row_update(boltzmann_affinity, column_factor):
    partial_rows = jnp.dot(boltzmann_affinity, column_factor, precision=lax.Precision.HIGHEST)
    totals = lax.psum(partial_rows, "cent")
    return 1.0 / totals


def shards(embeddings, centroids):
    normed = normalize(embeddings)
    cent_normed = normalize(centroids)
    cosine_matches = lax.dot_general(
        normed, cent_normed, (((1,), (1,)), ((), ())), preferred_element_type=jnp.float32
    )
    boltzmann_affinity = jnp.exp(cosine_matches * (1.0 / (FEATURE_DIM * entropy_regularizer)))
    local_cents = centroids.shape[0]
    row_count = embeddings.shape[0] * lax.axis_size("dp")
    cent_count = local_cents * lax.axis_size("cent")
    balance_ratio = row_count / cent_count
    column_factor = jnp.ones((local_cents,), jnp.float32)
    for sweep in range(ROUNDS):
        row_weight = row_update(boltzmann_affinity, column_factor)
        partial_cols = jnp.dot(row_weight, boltzmann_affinity, precision=lax.Precision.HIGHEST)
        column_factor = balance_ratio / lax.psum(partial_cols, "dp")
    row_weight = row_update(boltzmann_affinity, column_factor)
    transport = (row_weight[:, None] * boltzmann_affinity * column_factor[None, :]).astype(
        jnp.bfloat16
    )
    col_mass = jnp.sum(transport, axis=0, dtype=jnp.float32)
    own_rows = local_cents // lax.axis_size("dp")
    holder_position = lax.axis_index("dp")
    weighted = lax.dot_general(
        transport, normed, (((0,), (0,)), ((), ())), preferred_element_type=jnp.float32
    )
    weighted, col_mass = lax.psum((weighted, col_mass), "dp")
    weighted = lax.dynamic_slice_in_dim(weighted, holder_position * own_rows, own_rows, 0)
    col_mass = lax.dynamic_slice_in_dim(col_mass, holder_position * own_rows, own_rows, 0)
    return weighted / col_mass[:, None]


def solution(mesh):
    in_specs = (P("dp", None), P("cent", None))
    out_specs = P(("cent", "dp"), None)
    return jax.shard_map(shards, mesh=mesh, in_specs=in_specs, out_specs=out_specs, check_vma=False)
```

profile of v0, /device:TPU:1, one launch (start us, length us, event | category | flops | bytes accessed | tf_op | source)
XLA Modules:
  0.0 423.9 jit_solution(16495555627973379805)
XLA Ops:
  6.5 0.0 all-reduce.2.cloned.1.call-start
  6.5 1.4 fusion.4
  7.9 2.6 fusion
  10.5 4.1 multiply_exponential_fusion
  14.6 0.0 copy-start
  14.6 1.9 copy-done
  16.6 3.6 fusion.9
  20.2 15.0 %psum.49 = f32[512]{0:T(512)S(1)} all-reduce(f32[512]{0:T(512)S(1)} %bitcast.25), channel_id=1, replica_groups=mesh['dp'=32,'cent'=8] {'cent'}, use_global_device_ids=true, to_apply=%region_2.0 | all-reduce | flops 512 | bytes 4096 | tf_op jit(solution)/shard_map/psum | solution.py:19
  35.2 4.3 %fusion.12 = f32[1,2048]{1,0:T(1,128)S(1)} fusion(f32[512,1]{0,1:T(1,128)S(1)} %bitcast.22, f32[512,2048]{1,0:T(8,128)} %copy-done), kind=kOutput, calls=%fused_computation.24 | convolution fusion | flops 12582912 | bytes 4204544 | tf_op jit(solution)/shard_map/dot_general | solution.py:37
  39.4 63.4 %psum.50 = f32[2048]{0:T(1024)S(1)} all-reduce(f32[2048]{0:T(1024)S(1)} %bitcast.19), channel_id=1, replica_groups=mesh['dp'=32,'cent'=8] {'dp'}, use_global_device_ids=true, to_apply=%region_3.0 | all-reduce | flops 2048 | bytes 16384 | tf_op jit(solution)/shard_map/psum | solution.py:38
  102.9 5.8 %fusion.13 = f32[1,512]{1,0:T(1,128)S(1)} fusion(f32[512,2048]{1,0:T(8,128)} %copy-done, f32[2048,1]{0,1:T(1,128)S(1)} %bitcast.20), kind=kOutput, calls=%fused_computation.25 | convolution fusion | flops 12582912 | bytes 4204544 | tf_op jit(solution)/shard_map/dot_general | solution.py:18
  108.6 28.6 %psum.51 = f32[512]{0:T(512)S(1)} all-reduce(f32[512]{0:T(512)S(1)} %bitcast.23), channel_id=1, replica_groups=mesh['dp'=32,'cent'=8] {'cent'}, use_global_device_ids=true, to_apply=%region_4.0 | all-reduce | flops 512 | bytes 4096 | tf_op jit(solution)/shard_map/psum | solution.py:19
  137.2 0.0 copy-start.1
  137.2 4.3 %fusion.14 = f32[1,2048]{1,0:T(1,128)S(1)} fusion(f32[512,1]{0,1:T(1,128)S(1)} %bitcast.24, f32[512,2048]{1,0:T(8,128)} %copy-done), kind=kOutput, calls=%fused_computation.26 | convolution fusion | flops 12582912 | bytes 4204544 | tf_op jit(solution)/shard_map/dot_general | solution.py:37
  141.6 57.2 %psum.52 = f32[2048]{0:T(1024)S(1)} all-reduce(f32[2048]{0:T(1024)S(1)} %bitcast.21), channel_id=1, replica_groups=mesh['dp'=32,'cent'=8] {'dp'}, use_global_device_ids=true, to_apply=%region_5.0 | all-reduce | flops 2048 | bytes 16384 | tf_op jit(solution)/shard_map/psum | solution.py:38
  198.8 5.8 %fusion.15 = f32[1,512]{1,0:T(1,128)S(1)} fusion(f32[512,2048]{1,0:T(8,128)} %copy-done, f32[2048,1]{0,1:T(1,128)S(1)} %bitcast.18), kind=kOutput, calls=%fused_computation.27 | convolution fusion | flops 12582912 | bytes 4204544 | tf_op jit(solution)/shard_map/dot_general | solution.py:18
  204.6 25.8 %psum.53 = f32[512]{0:T(512)S(1)} all-reduce(f32[512]{0:T(512)S(1)} %bitcast.26), channel_id=1, replica_groups=mesh['dp'=32,'cent'=8] {'cent'}, use_global_device_ids=true, to_apply=%region_6.0 | all-reduce | flops 512 | bytes 4096 | tf_op jit(solution)/shard_map/psum | solution.py:19
  230.4 0.0 copy-done.1
  230.4 6.8 %fusion.6 = f32[2048,768]{1,0:T(8,128)} fusion(bf16[512,768]{1,0:T(8,128)(2,1)S(1)} %copy-done.1, f32[512]{0:T(512)S(1)} %add_rsqrt_fusion.1, f32[512,2048]{1,0:T(8,128)} %copy-done, f32[2048]{0:T(1024)S(1)} %broadcast_divide_fusion.1, f32[512]{0:T(512)S(1)} %broadcast_divide_fusion.2), kind=kOutput, calls=%fused_computation.12 | convolution fusion | flops 1614938112 | bytes 11284480 | tf_op jit(solution)/shard_map/dot_general | solution.py:46
  237.3 0.0 all-reduce.2.cloned.1.call-update
  237.3 2.7 convert_reduce_fusion
  240.0 62.2 %psum.55 = f32[2048]{0:T(1024)S(1)} all-reduce(f32[2048]{0:T(1024)S(1)} %convert_reduce_fusion), channel_id=1, replica_groups=mesh['dp'=32,'cent'=8] {'dp'}, use_global_device_ids=true, to_apply=%region_9.0 | all-reduce | flops 2048 | bytes 16384 | tf_op jit(solution)/shard_map/psum | solution.py:49
  302.2 0.1 dynamic_slice.7
  302.3 113.1 %all-reduce.2.cloned.1.call-done = f32[2048,768]{1,0:T(8,128)} async-done(((f32[2048,768]{1,0:T(8,128)}), f32[2048,768]{1,0:T(8,128)}) %all-reduce.2.cloned.1.call-update) | async-done | bytes 6291472 | tf_op jit(solution)/shard_map/psum | solution.py:49
  415.3 1.7 dynamic-slice_divide_fusion
  (7 shorter events, 0.0 us)
Async XLA Ops:
  6.5 408.8 %all-reduce.2.cloned.1.call-start = ((), (), s32[]{:S(2)}) async-start(), calls=%async_computation | async-start | bytes 12582912 | tf_op jit(solution)/shard_map/psum | solution.py:49
  14.6 2.0 copy-start
  137.2 93.2 %copy-start.1 = (bf16[512,768]{1,0:T(8,128)(2,1)S(1)}, bf16[512,768]{1,0:T(8,128)(2,1)}, u32[]{:S(2)}) copy-start(bf16[512,768]{1,0:T(8,128)(2,1)} %param.2) | copy-start | bytes 2359300
Sparse Core Ops, SparseCore 0:
  237.4 177.8 all-reduce.1
where the time goes:
time: 424 us
  blocking collectives  252 us (59%)
  waiting for transfers between devices  113 us (27%)
  matrix products  34.7 us (8%)
  between operations  13.5 us (3%)
  other arithmetic  8.35 us (2%)
    psum x2, blocking collectives, shards(): column_factor = balance_ratio / lax.psum(partial_cols, 'dp')  121 us
    psum x1, waiting for transfers between devices, shards(): weighted, col_mass = lax.psum((weighted, col_mass), 'dp')  113 us
    psum x3, blocking collectives, row_update(): totals = lax.psum(partial_rows, 'cent')  69.4 us
    psum x1, blocking collectives, shards(): weighted, col_mass = lax.psum((weighted, col_mass), 'dp')  62.2 us
    dot_general x3, matrix products, row_update(): jnp.dot(boltzmann_affinity, column_factor, precision=lax.Precision.HIGHEST)  15.1 us
    dot_general x2, matrix products, shards(): jnp.dot(row_weight, boltzmann_affinity, precision=lax.Precision.HIGHEST)  8.61 us
  transfers between devices with their start and end apart: 1, of which 1 were waited for; matrix products, arithmetic and copies ran while one was open for 1% of the time, Pallas kernels for 0%

commit v1 on v0

--- a/solution.py
+++ b/solution.py
@@ -35,7 +35,7 @@
     for sweep in range(ROUNDS):
         row_weight = row_update(boltzmann_affinity, column_factor)
         partial_cols = jnp.dot(row_weight, boltzmann_affinity, precision=lax.Precision.HIGHEST)
-        column_factor = balance_ratio / lax.psum(partial_cols, "dp")
+        column_factor = balance_ratio / jnp.sum(lax.all_gather(partial_cols, "dp"), axis=0)
     row_weight = row_update(boltzmann_affinity, column_factor)
     transport = (row_weight[:, None] * boltzmann_affinity * column_factor[None, :]).astype(
         jnp.bfloat16

time: 424 us -> 379 us (0.89)
  blocking collectives: 252 us -> 204 us
    psum x2 -> x0, blocking collectives: 121 us -> none  [shards(): column_factor = balance_ratio / lax.psum(partial_cols, 'dp')]
    all_gather x0 -> x2, blocking collectives: none -> 74.4 us  [shards(): lax.all_gather(partial_cols, 'dp')]
where the time goes in v1:
time: 379 us; the launch traced here: 378 us
  blocking collectives  204 us (54%)
  waiting for transfers between devices  115 us (30%)
  matrix products  34.7 us (9%)
  between operations  13.5 us (4%)
  other arithmetic  8.41 us (2%)
    psum x1, waiting for transfers between devices, shards(): weighted, col_mass = lax.psum((weighted, col_mass), 'dp')  115 us
    all_gather x2, blocking collectives, shards(): lax.all_gather(partial_cols, 'dp')  74.4 us
    psum x3, blocking collectives, row_update(): totals = lax.psum(partial_rows, 'cent')  67 us
    psum x1, blocking collectives, shards(): weighted, col_mass = lax.psum((weighted, col_mass), 'dp')  62.5 us
    dot_general x3, matrix products, row_update(): jnp.dot(boltzmann_affinity, column_factor, precision=lax.Precision.HIGHEST)  15.1 us
    dot_general x2, matrix products, shards(): jnp.dot(row_weight, boltzmann_affinity, precision=lax.Precision.HIGHEST)  8.61 us
  transfers between devices with their start and end apart: 1, of which 1 were waited for; matrix products, arithmetic and copies ran while one was open for 1% of the time, Pallas kernels for 0%

profile of v1, /device:TPU:1, one launch (start us, length us, event | category | flops | bytes accessed | tf_op | source)
XLA Modules:
  0.0 378.1 jit_solution(13290354889377410753)
XLA Ops:
  6.5 0.0 all-reduce.2.cloned.1.call-start
  6.5 1.4 fusion.4
  7.9 2.6 fusion
  10.5 4.1 %multiply_exponential_fusion = f32[512,2048]{1,0:T(8,128)S(1)} fusion(bf16[2048,768]{1,0:T(8,128)(2,1)} %param.3, f32[2048]{0:T(1024)S(1)} %add_rsqrt_fusion, bf16[512,768]{1,0:T(8,128)(2,1)} %param.2, f32[512]{0:T(512)S(1)} %add_rsqrt_fusion.1), kind=kOutput, calls=%fused_computation.6 | convolution fusion | flops 1617559552 | bytes 8136704 | tf_op jit(solution)/shard_map/dot_general | solution.py:26
  14.6 0.0 copy-start
  14.6 1.9 copy-done
  16.6 3.6 fusion.9
  20.2 15.0 %psum.35 = f32[512]{0:T(512)S(1)} all-reduce(f32[512]{0:T(512)S(1)} %bitcast.25), channel_id=1, replica_groups=mesh['dp'=32,'cent'=8] {'cent'}, use_global_device_ids=true, to_apply=%region_2.0 | all-reduce | flops 512 | bytes 4096 | tf_op jit(solution)/shard_map/psum | solution.py:19
  35.2 4.3 %fusion.12 = f32[1,2048]{1,0:T(1,128)S(1)} fusion(f32[512,1]{0,1:T(1,128)S(1)} %bitcast.22, f32[512,2048]{1,0:T(8,128)} %copy-done), kind=kOutput, calls=%fused_computation.24 | convolution fusion | flops 12582912 | bytes 4204544 | tf_op jit(solution)/shard_map/dot_general | solution.py:37
  39.4 38.5 %all-gather = f32[65536]{0:T(1024)S(1)} all-gather(f32[2048]{0:T(1024)S(1)} %bitcast.19), channel_id=2, replica_groups=mesh['dp'=32,'cent'=8] {'dp'}, dimensions={0}, use_global_device_ids=true | all-gather | bytes 270336 | tf_op jit(solution)/shard_map/all_gather | solution.py:38
  78.0 5.8 %fusion.13 = f32[1,512]{1,0:T(1,128)S(1)} fusion(f32[512,2048]{1,0:T(8,128)} %copy-done, f32[2048,1]{0,1:T(1,128)S(1)} %bitcast.21), kind=kOutput, calls=%fused_computation.25 | convolution fusion | flops 12582912 | bytes 4204544 | tf_op jit(solution)/shard_map/dot_general | solution.py:18
  83.8 27.2 %psum.36 = f32[512]{0:T(512)S(1)} all-reduce(f32[512]{0:T(512)S(1)} %bitcast.23), channel_id=1, replica_groups=mesh['dp'=32,'cent'=8] {'cent'}, use_global_device_ids=true, to_apply=%region_4.0 | all-reduce | flops 512 | bytes 4096 | tf_op jit(solution)/shard_map/psum | solution.py:19
  111.0 0.0 copy-start.1
  111.0 4.3 %fusion.14 = f32[1,2048]{1,0:T(1,128)S(1)} fusion(f32[512,1]{0,1:T(1,128)S(1)} %bitcast.24, f32[512,2048]{1,0:T(8,128)} %copy-done), kind=kOutput, calls=%fused_computation.26 | convolution fusion | flops 12582912 | bytes 4204544 | tf_op jit(solution)/shard_map/dot_general | solution.py:37
  115.4 35.9 %all-gather.1 = f32[65536]{0:T(1024)S(1)} all-gather(f32[2048]{0:T(1024)S(1)} %bitcast.20), channel_id=3, replica_groups=mesh['dp'=32,'cent'=8] {'dp'}, dimensions={0}, use_global_device_ids=true | all-gather | bytes 270336 | tf_op jit(solution)/shard_map/all_gather | solution.py:38
  151.4 5.8 %fusion.15 = f32[1,512]{1,0:T(1,128)S(1)} fusion(f32[512,2048]{1,0:T(8,128)} %copy-done, f32[2048,1]{0,1:T(1,128)S(1)} %bitcast.18), kind=kOutput, calls=%fused_computation.27 | convolution fusion | flops 12582912 | bytes 4204544 | tf_op jit(solution)/shard_map/dot_general | solution.py:18
  157.2 24.7 %psum.37 = f32[512]{0:T(512)S(1)} all-reduce(f32[512]{0:T(512)S(1)} %bitcast.26), channel_id=1, replica_groups=mesh['dp'=32,'cent'=8] {'cent'}, use_global_device_ids=true, to_apply=%region_6.0 | all-reduce | flops 512 | bytes 4096 | tf_op jit(solution)/shard_map/psum | solution.py:19
  181.9 0.0 copy-done.1
  181.9 6.8 %fusion.6 = f32[2048,768]{1,0:T(8,128)} fusion(bf16[512,768]{1,0:T(8,128)(2,1)S(1)} %copy-done.1, f32[512]{0:T(512)S(1)} %add_rsqrt_fusion.1, f32[512,2048]{1,0:T(8,128)} %copy-done, f32[2048]{0:T(1024)S(1)} %broadcast_divide_fusion.1, f32[512]{0:T(512)S(1)} %broadcast_divide_fusion.2), kind=kOutput, calls=%fused_computation.12 | convolution fusion | flops 1614938112 | bytes 11284480 | tf_op jit(solution)/shard_map/dot_general | solution.py:46
  188.8 0.0 all-reduce.2.cloned.1.call-update
  188.8 2.7 convert_reduce_fusion
  191.5 62.5 %psum.39 = f32[2048]{0:T(1024)S(1)} all-reduce(f32[2048]{0:T(1024)S(1)} %convert_reduce_fusion), channel_id=1, replica_groups=mesh['dp'=32,'cent'=8] {'dp'}, use_global_device_ids=true, to_apply=%region_9.0 | all-reduce | flops 2048 | bytes 16384 | tf_op jit(solution)/shard_map/psum | solution.py:49
  254.0 0.1 dynamic_slice.7
  254.1 115.4 %all-reduce.2.cloned.1.call-done = f32[2048,768]{1,0:T(8,128)} async-done(((f32[2048,768]{1,0:T(8,128)}), f32[2048,768]{1,0:T(8,128)}) %all-reduce.2.cloned.1.call-update) | async-done | bytes 6291472 | tf_op jit(solution)/shard_map/psum | solution.py:49
  369.5 1.7 dynamic-slice_divide_fusion
  (11 shorter events, 0.2 us)
Async XLA Ops:
  6.5 363.0 %all-reduce.2.cloned.1.call-start = ((), (), s32[]{:S(2)}) async-start(), calls=%async_computation | async-start | bytes 12582912 | tf_op jit(solution)/shard_map/psum | solution.py:49
  14.6 2.0 copy-start
  111.0 70.9 %copy-start.1 = (bf16[512,768]{1,0:T(8,128)(2,1)S(1)}, bf16[512,768]{1,0:T(8,128)(2,1)}, u32[]{:S(2)}) copy-start(bf16[512,768]{1,0:T(8,128)(2,1)} %param.2) | copy-start | bytes 2359300
Sparse Core Ops, SparseCore 0:
  188.9 180.5 all-reduce.1
